TPU v7x, 256 devices: a whole 4x4x8 slice. The times are simulated.
256 devices in a mesh: mp: 32 (over z, y_hi, core), dp: 8 (over x, y_lo).
Axes of the slice: x: 4, y: 4 (y_hi: 2, y_lo: 2; y = y_hi * 2 + y_lo), z: 8, core: 2. Of those that a mesh axis runs over, the one named last changes fastest.
Arguments:
- tokens: bfloat16 [1024, 8192], P('mp', 'dp'), may hold values from -6 to 6
- gate_weight: bfloat16 [8192, 16384], P('dp', 'mp'), may hold values from -0.0625 to 0.0625
- up_weight: bfloat16 [8192, 16384], P('dp', 'mp'), may hold values from -0.0625 to 0.0625
- down_weight: bfloat16 [16384, 8192], P('mp', 'dp'), may hold values from -0.046875 to 0.046875
- cotangent: bfloat16 [1024, 8192], P('mp', 'dp'), may hold values from -6 to 6
Outputs:
- mixed: bfloat16 [1024, 8192], P('mp', 'dp')
- token_grad: bfloat16 [1024, 8192], P('mp', 'dp')
- gate_grad: bfloat16 [8192, 16384], P('dp', 'mp')
- up_grad: bfloat16 [8192, 16384], P('dp', 'mp')
- down_grad: bfloat16 [16384, 8192], P('mp', 'dp')
All inputs are finite; a program needn't handle non-finite values.
Results may differ from a plain program's by a relative error of at most 0.005.
Values may be sent and summed in bfloat16 or wider, within the bound.
No kernel may reach another device: no remote copies, remote signals or barrier semaphores. Data moves between devices by JAX's collectives and lax.ppermute only.
A program may use at most 64 MiB of HBM per device.

v0:
```python
import jax
import jax.numpy as jnp
from jax import lax
from jax.sharding import PartitionSpec as P


def contract_rows(left, right):
    return lax.dot_general(
        left, right, (((0,), (0,)), ((), ())), preferred_element_type=jnp.float32
    )


def contract_cols(left, right):
    return lax.dot_general(
        left, right, (((1,), (1,)), ((), ())), preferred_element_type=jnp.float32
    )


def body(tokens, gate_weight, up_weight, down_weight, cotangent):
    token_all = lax.all_gather(tokens, "mp", axis=0, tiled=True)
    width = gate_weight.shape[1]
    block = token_all
    first = jnp.dot(block, gate_weight, preferred_element_type=jnp.float32)
    second = jnp.dot(block, up_weight, preferred_element_type=jnp.float32)
    both = lax.psum(jnp.concatenate([first, second], axis=1), "dp")
    gate = both[:, :width]
    up = both[:, width:]
    sig = jax.nn.sigmoid(gate)
    act = gate * sig
    hidden_part = (act * up).astype(jnp.bfloat16)
    block = hidden_part
    mixed = lax.psum_scatter(
        jnp.dot(block, down_weight, preferred_element_type=jnp.float32),
        "mp",
        scatter_dimension=0,
        tiled=True,
    ).astype(jnp.bfloat16)
    cot_all = lax.all_gather(cotangent, "mp", axis=0, tiled=True)
    down_grad = contract_rows(hidden_part, cot_all).astype(jnp.bfloat16)
    block = cot_all
    hidden_back = lax.psum(contract_cols(block, down_weight), "dp")
    pre_gate = (hidden_back * up * sig * (1.0 + gate * (1.0 - sig))).astype(jnp.bfloat16)
    pre_up = (hidden_back * act).astype(jnp.bfloat16)
    gate_all, up_all = (pre_gate, pre_up)
    gate_grad = contract_rows(token_all, gate_all).astype(jnp.bfloat16)
    up_grad = contract_rows(token_all, up_all).astype(jnp.bfloat16)
    first = gate_all
    second = up_all
    token_grad = lax.psum_scatter(
        contract_cols(first, gate_weight) + contract_cols(second, up_weight),
        "mp",
        scatter_dimension=0,
        tiled=True,
    ).astype(jnp.bfloat16)
    return (mixed, token_grad, gate_grad, up_grad, down_grad)


def solution(mesh):
    in_specs = (P("mp", "dp"), P("dp", "mp"), P("dp", "mp"), P("mp", "dp"), P("mp", "dp"))
    out_specs = (P("mp", "dp"), P("mp", "dp"), P("dp", "mp"), P("dp", "mp"), P("mp", "dp"))
    return jax.shard_map(body, mesh=mesh, in_specs=in_specs, out_specs=out_specs, check_vma=False)
```

profile of v0, /device:TPU:6, one launch (start us, length us, event | category | flops | bytes accessed | tf_op | source)
XLA Modules:
  0.0 717.8 jit_solution(3119205423730051404)
XLA Ops:
  7.2 0.0 copy-start
  7.2 0.0 all-gather.3.cloned.1.call-start
  7.2 0.7 all-gather.3.cloned.1.call-update
  7.9 0.0 all-gather.5.cloned.1.call-start
  8.0 0.7 all-gather.5.cloned.1.call-update
  8.7 0.0 all-reduce.3.cloned.1.call-start
  8.7 84.9 %all-gather.3.cloned.1.call-done = bf16[1024,1024]{1,0:T(8,128)(2,1)} async-done(((bf16[32,1024]{1,0:T(8,128)(2,1)}), bf16[1024,1024]{1,0:T(8,128)(2,1)}) %all-gather.3.cloned.1.call-update) | async-done | bytes 2097168 | tf_op jit(solution)/shard_map/all_gather | solution.py:20
  93.6 3.3 fusion.4
  96.9 1.3 fusion.3
  98.2 2.5 pad_maximum_fusion
  100.7 72.0 %all-gather.5.cloned.1.call-done = bf16[1024,1024]{1,0:T(8,128)(2,1)} async-done(((bf16[32,1024]{1,0:T(8,128)(2,1)}), bf16[1024,1024]{1,0:T(8,128)(2,1)}) %all-gather.5.cloned.1.call-update) | async-done | bytes 2097168 | tf_op jit(solution)/shard_map/all_gather | solution.py:38
  172.7 4.2 fusion.6
  176.9 0.0 all-reduce.3.cloned.1.call-update
  176.9 0.0 reduce-scatter.5.cloned.1.call-start
  177.0 262.9 %all-reduce.3.cloned.1.call-done = (f32[1024,1024]{0,1:T(8,128)}, f32[1024,512]{0,1:T(8,128)}) async-done(((f32[1024,1024]{0,1:T(8,128)}, f32[1024,512]{0,1:T(8,128)}), (f32[1024,1024]{0,1:T(8,128)}, f32[1024,512]{0,1:T(8,128)})) %all-reduce.3.cloned.1.call-update) | async-done | bytes 6291472 | tf_op jit(solution)/shard_map/psum | solution.py:25
  439.9 4.3 multiply_convert_fusion
  444.2 1.3 fusion.7
  445.5 0.3 copy-done.1
  445.8 3.3 convolution_add_fusion
  449.1 0.0 reduce-scatter.5.cloned.1.call-update
  449.1 0.2 reduce-scatter.3.cloned.1.call-start
  449.3 4.5 fusion.5
  453.8 0.0 reduce-scatter.3.cloned.1.call-update
  453.8 4.1 fusion.1
  458.0 2.3 copy.11
  460.3 3.8 fusion.2
  464.1 2.3 copy.12
  466.4 3.9 convolution_convert_fusion
  470.2 109.2 %reduce-scatter.5.cloned.1.call-done = f32[32,1024]{1,0:T(8,128)} async-done(((f32[1024,1024]{1,0:T(8,128)}), f32[32,1024]{1,0:T(8,128)}) %reduce-scatter.5.cloned.1.call-update) | async-done | bytes 131088 | tf_op jit(solution)/shard_map/reduce_scatter | solution.py:49
  579.4 1.5 convert_element_type.34
  581.0 128.8 %reduce-scatter.3.cloned.1.call-done = f32[32,1024]{1,0:T(8,128)} async-done(((f32[1024,1024]{1,0:T(8,128)}), f32[32,1024]{1,0:T(8,128)}) %reduce-scatter.3.cloned.1.call-update) | async-done | bytes 131088 | tf_op jit(solution)/shard_map/reduce_scatter | solution.py:32
  709.8 1.5 convert_element_type.31
  (8 shorter events, 0.0 us)
Async XLA Ops:
  7.2 89.7 %copy-start = (bf16[1024,512]{1,0:T(8,128)(2,1)S(1)}, bf16[1024,512]{1,0:T(8,128)(2,1)}, u32[]{:S(2)}) copy-start(bf16[1024,512]{1,0:T(8,128)(2,1)} %param.6) | copy-start | bytes 3145732
  7.2 86.4 %all-gather.3.cloned.1.call-start = ((), (), s32[]{:S(2)}) async-start(), calls=%async_computation.2 | async-start | bytes 2162688 | tf_op jit(solution)/shard_map/all_gather | solution.py:20
  7.9 164.8 %all-gather.5.cloned.1.call-start = ((), (), s32[]{:S(2)}) async-start(), calls=%async_computation.4 | async-start | bytes 2162688 | tf_op jit(solution)/shard_map/all_gather | solution.py:38
  8.7 431.2 %all-reduce.3.cloned.1.call-start = ((), (), s32[]{:S(2)}) async-start(), calls=%async_computation.6 | async-start | bytes 12582912 | tf_op jit(solution)/shard_map/psum | solution.py:25
  93.6 3.3 copy-start.4
  98.2 74.5 %copy-start.3 = (bf16[512,1024]{1,0:T(8,128)(2,1)S(1)}, bf16[512,1024]{1,0:T(8,128)(2,1)}, u32[]{:S(2)}) copy-start(bf16[512,1024]{1,0:T(8,128)(2,1)} %param.8) | copy-start | bytes 3145732
  176.9 402.5 %reduce-scatter.5.cloned.1.call-start = ((), (), s32[]{:S(2)}) async-start(), calls=%async_computation.5 | async-start | bytes 4325376 | tf_op jit(solution)/shard_map/reduce_scatter | solution.py:49
  444.2 1.3 copy-start.2
  444.2 1.6 copy-start.1
  449.1 260.7 %reduce-scatter.3.cloned.1.call-start = ((), (), s32[]{:S(2)}) async-start(), calls=%async_computation.3 | async-start | bytes 4325376 | tf_op jit(solution)/shard_map/reduce_scatter | solution.py:32
Sparse Core Ops, SparseCore 0:
  10.8 82.7 all-gather.2
  96.4 76.3 all-gather.4
  177.1 262.8 all-reduce.2
  449.2 130.1 reduce-scatter.4
  583.5 126.2 reduce-scatter.2
where the time goes:
time: 718 us
  waiting for transfers between devices  659 us (92%)
  matrix products  29.7 us (4%)
  between operations  13.9 us (2%)
  other arithmetic  9.84 us (1%)
    psum x1, waiting for transfers between devices, body(): both = lax.psum(jnp.concatenate([first, second], axis=1), 'dp')  263 us
    reduce_scatter x1, waiting for transfers between devices, body(): lax.psum_scatter(jnp.dot(block, down_weight, preferred_element_type=jnp.f...  129 us
    reduce_scatter x1, waiting for transfers between devices, body(): lax.psum_scatter(contract_cols(first, gate_weight) + contract_cols(second...  109 us
    all_gather x1, waiting for transfers between devices, body(): token_all = lax.all_gather(tokens, 'mp', axis=0, tiled=True)  84.9 us
    all_gather x1, waiting for transfers between devices, body(): cot_all = lax.all_gather(cotangent, 'mp', axis=0, tiled=True)  72 us
  transfers between devices with their start and end apart: 5, of which 5 were waited for; matrix products, arithmetic and copies ran while one was open for 4% of the time, Pallas kernels for 0%

commit v1 on v0

--- a/solution.py
+++ b/solution.py
@@ -22,7 +22,9 @@
     block = token_all
     first = jnp.dot(block, gate_weight, preferred_element_type=jnp.float32)
     second = jnp.dot(block, up_weight, preferred_element_type=jnp.float32)
-    both = lax.psum(jnp.concatenate([first, second], axis=1), "dp")
+    part = jnp.concatenate([first, second], axis=1)
+    pieces = lax.all_gather(part, "dp")
+    both = jnp.sum(pieces, axis=0)
     gate = both[:, :width]
     up = both[:, width:]
     sig = jax.nn.sigmoid(gate)

time: 718 us -> 1200 us (1.67)
  waiting for transfers between devices: 659 us -> 1090 us
  local copies, waits for them, and re-layouts: 4.87 us -> 48.6 us
  other arithmetic: 9.84 us -> 22.5 us
    all_gather x0 -> x1, waiting for transfers between devices: none -> 637 us  [body(): pieces = lax.all_gather(part, 'dp')]
    psum x1, waiting for transfers between devices: 263 us -> 56.6 us  [body(): hidden_back = lax.psum(contract_cols(block, down_weight), 'dp')]
    unnamed x12 -> x17, local copies, waits for them, and re-layouts: 4.87 us -> 44.5 us
    reduce_sum x0 -> x1, other arithmetic: none -> 12.6 us  [body(): both = jnp.sum(pieces, axis=0)]
  transfers between devices with their start and end apart: 5 -> 6, of which waited for: 5 -> 6; matrix products, arithmetic and copies ran while one was open for 4% -> 7% of each run, Pallas kernels for 0% -> 0%
where the time goes in v1:
time: 1200 us
  waiting for transfers between devices  1090 us (91%)
  local copies, waits for them, and re-layouts  48.6 us (4%)
  matrix products  29.5 us (2%)
  other arithmetic  22.5 us (2%)
  between operations  14.2 us (1%)
    all_gather x1, waiting for transfers between devices, body(): pieces = lax.all_gather(part, 'dp')  637 us
    reduce_scatter x1, waiting for transfers between devices, body(): lax.psum_scatter(jnp.dot(block, down_weight, preferred_element_type=jnp.f...  129 us
    reduce_scatter x1, waiting for transfers between devices, body(): lax.psum_scatter(contract_cols(first, gate_weight) + contract_cols(second...  108 us
    all_gather x1, waiting for transfers between devices, body(): token_all = lax.all_gather(tokens, 'mp', axis=0, tiled=True)  84.9 us
    all_gather x1, waiting for transfers between devices, body(): cot_all = lax.all_gather(cotangent, 'mp', axis=0, tiled=True)  72.1 us
    psum x1, waiting for transfers between devices, body(): hidden_back = lax.psum(contract_cols(block, down_weight), 'dp')  56.6 us
    unnamed x17, local copies, waits for them, and re-layouts  44.5 us
  transfers between devices with their start and end apart: 6, of which 6 were waited for; matrix products, arithmetic and copies ran while one was open for 7% of the time, Pallas kernels for 0%

profile of v1, /device:TPU:6, one launch (start us, length us, event | category | flops | bytes accessed | tf_op | source)
XLA Modules:
  0.0 1203.9 jit_solution(17300734887827706169)
XLA Ops:
  7.2 0.7 all-gather.5.cloned.1.call-update
  8.0 0.7 all-gather.7.cloned.1.call-update
  8.7 84.9 %all-gather.5.cloned.1.call-done = bf16[1024,1024]{1,0:T(8,128)(2,1)} async-done(((bf16[32,1024]{1,0:T(8,128)(2,1)}), bf16[1024,1024]{1,0:T(8,128)(2,1)}) %all-gather.5.cloned.1.call-update) | async-done | bytes 2097168 | tf_op jit(solution)/shard_map/all_gather | solution.py:20
  93.6 3.0 fusion.4
  96.6 1.3 fusion.5
  98.0 2.6 pad_maximum_fusion
  100.6 0.0 all-reduce.2.cloned.1.call-start
  100.6 72.1 %all-gather.7.cloned.1.call-done = bf16[1024,1024]{1,0:T(8,128)(2,1)} async-done(((bf16[32,1024]{1,0:T(8,128)(2,1)}), bf16[1024,1024]{1,0:T(8,128)(2,1)}) %all-gather.7.cloned.1.call-update) | async-done | bytes 2097168 | tf_op jit(solution)/shard_map/all_gather | solution.py:40
  172.7 4.2 fusion.7
  176.9 0.2 reduce-scatter.5.cloned.1.call-start
  177.2 636.6 %all-gather.9.cloned.1.call-done = f32[8192,1024]{0,1:T(8,128)} async-done(((f32[1024,1024]{0,1:T(8,128)}), f32[8192,1024]{0,1:T(8,128)}) %all-gather.9.cloned.1.call-update) | async-done | bytes 33554448 | tf_op jit(solution)/shard_map/all_gather | solution.py:26
  813.8 34.9 %copy.18 = f32[128,8,8,1024]{3,2,1,0:T(8,128)S(1)} copy(f32[128,8,8,1024]{3,1,2,0:T(8,128)} %bitcast.27) | data formatting | bytes 67108864
  848.7 12.6 %bitcast_reduce_fusion = f32[1024,1024]{0,1:T(8,128)} fusion(f32[128,8,8,1024]{3,2,1,0:T(8,128)S(1)} %copy.18), kind=kLoop, calls=%fused_computation | loop fusion | flops 7340032 | bytes 37748736 | tf_op jit(solution)/shard_map/reduce_sum | solution.py:27
  861.3 4.0 fusion.3
  865.3 2.9 copy.16
  868.2 1.8 copy.17
  870.0 56.6 %all-reduce.2.cloned.1.call-done = f32[1024,512]{1,0:T(8,128)} async-done(((f32[1024,512]{1,0:T(8,128)}), f32[1024,512]{1,0:T(8,128)}) %all-reduce.2.cloned.1.call-update) | async-done | bytes 2097168 | tf_op jit(solution)/shard_map/psum | solution.py:43
  926.6 4.2 multiply_convert_fusion
  930.9 1.3 fusion.8
  932.2 0.3 copy-done.4
  932.5 3.3 convolution_add_fusion
  935.8 0.3 reduce-scatter.3.cloned.1.call-start
  936.1 4.4 fusion.6
  940.6 4.2 fusion.1
  944.7 2.3 copy.14
  947.0 3.9 fusion.2
  950.9 2.3 copy.15
  953.2 3.9 convolution_convert_fusion
  957.0 108.2 %reduce-scatter.5.cloned.1.call-done = f32[32,1024]{1,0:T(8,128)} async-done(((f32[1024,1024]{1,0:T(8,128)}), f32[32,1024]{1,0:T(8,128)}) %reduce-scatter.5.cloned.1.call-update) | async-done | bytes 131088 | tf_op jit(solution)/shard_map/reduce_scatter | solution.py:51
  1065.2 1.5 convert_element_type.34
  1066.7 128.8 %reduce-scatter.3.cloned.1.call-done = f32[32,1024]{1,0:T(8,128)} async-done(((f32[1024,1024]{1,0:T(8,128)}), f32[32,1024]{1,0:T(8,128)}) %reduce-scatter.3.cloned.1.call-update) | async-done | bytes 131088 | tf_op jit(solution)/shard_map/reduce_scatter | solution.py:34
  1195.5 1.5 convert_element_type.31
  (18 shorter events, 0.2 us)
Async XLA Ops:
  7.2 86.4 %copy-start = (bf16[1024,512]{1,0:T(8,128)(2,1)S(1)}, bf16[1024,512]{1,0:T(8,128)(2,1)}, u32[]{:S(2)}) copy-start(bf16[1024,512]{1,0:T(8,128)(2,1)} %param.6) | copy-start | bytes 3145732
  7.2 86.4 %all-gather.5.cloned.1.call-start = ((), (), s32[]{:S(2)}) async-start(), calls=%async_computation.2 | async-start | bytes 2162688 | tf_op jit(solution)/shard_map/all_gather | solution.py:20
  7.9 164.8 %all-gather.7.cloned.1.call-start = ((), (), s32[]{:S(2)}) async-start(), calls=%async_computation.4 | async-start | bytes 2162688 | tf_op jit(solution)/shard_map/all_gather | solution.py:40
  8.7 88.0 %copy-start.3 = (bf16[1024,512]{1,0:T(8,128)(2,1)S(1)}, bf16[1024,512]{1,0:T(8,128)(2,1)}, u32[]{:S(2)}) copy-start(bf16[1024,512]{1,0:T(8,128)(2,1)} %param.7) | copy-start | bytes 3145732
  8.7 805.1 %all-gather.9.cloned.1.call-start = ((), (), s32[]{:S(2)}) async-start(), calls=%async_computation.7 | async-start | bytes 37748736 | tf_op jit(solution)/shard_map/all_gather | solution.py:26
  93.6 3.0 copy-start.1
  100.6 72.2 %copy-start.5 = (bf16[512,1024]{1,0:T(8,128)(2,1)S(1)}, bf16[512,1024]{1,0:T(8,128)(2,1)}, u32[]{:S(2)}) copy-start(bf16[512,1024]{1,0:T(8,128)(2,1)} %param.8) | copy-start | bytes 3145732
  100.6 826.1 %all-reduce.2.cloned.1.call-start = ((), (), s32[]{:S(2)}) async-start(), calls=%async_computation.5 | async-start | bytes 4194304 | tf_op jit(solution)/shard_map/psum | solution.py:43
  176.9 888.3 %reduce-scatter.5.cloned.1.call-start = ((), (), s32[]{:S(2)}) async-start(), calls=%async_computation.6 | async-start | bytes 4325376 | tf_op jit(solution)/shard_map/reduce_scatter | solution.py:51
  930.9 1.3 copy-start.2
  930.9 1.6 copy-start.4
  935.8 259.7 %reduce-scatter.3.cloned.1.call-start = ((), (), s32[]{:S(2)}) async-start(), calls=%async_computation.3 | async-start | bytes 4325376 | tf_op jit(solution)/shard_map/reduce_scatter | solution.py:34
Sparse Core Ops, SparseCore 0:
  10.8 82.7 all-gather.4
  96.4 76.3 all-gather.6
  174.5 639.2 all-gather.8
  816.3 110.2 all-reduce.1
  936.0 129.1 reduce-scatter.4
  1069.3 126.1 reduce-scatter.2
